TPU v7x, 32 devices: a whole 2x2x4 slice. The times are simulated.
32 devices in a mesh: dp: 8 (over y, x, core), tensor: 4 (over z).
Axes of the slice: x: 2, y: 2, z: 4, core: 2. Of those that a mesh axis runs over, the one named last changes fastest.
Arguments:
- layer_input: bfloat16 [2048, 8, 768], P('tensor', 'dp'), may hold values from -6 to 6
- segments: int32 [8, 2048], P('dp'), may hold values from 0 to 64, as said below
- qkv_weight: bfloat16 [768, 2304], P(None, 'tensor'), may hold values from -0.21875 to 0.21875
- out_weight: bfloat16 [768, 768], P('tensor'), may hold values from -1.25 to 1.25
- gate_weight: bfloat16 [768, 3072], P(None, 'tensor'), may hold values from -0.21875 to 0.21875
- up_weight: bfloat16 [768, 3072], P(None, 'tensor'), may hold values from -0.21875 to 0.21875
- down_weight: bfloat16 [3072, 768], P('tensor'), may hold values from -0.109375 to 0.109375
- norm_params: float32 [4, 768], replicated, may hold values from -1.2 to 1.5, as said below
- cotangent: bfloat16 [2048, 8, 768], P('tensor', 'dp'), may hold values from -6 to 6
Outputs:
- layer_output: bfloat16 [2048, 8, 768], P('tensor', 'dp')
- input_grad: float32 [2048, 8, 768], P('tensor', 'dp')
- qkv_grad: float32 [768, 2304], P(None, 'tensor')
- out_grad: float32 [768, 768], P('tensor')
- gate_grad: float32 [768, 3072], P(None, 'tensor')
- up_grad: float32 [768, 3072], P(None, 'tensor')
- down_grad: float32 [3072, 768], P('tensor')
- norm_grads: float32 [4, 768], replicated
Inputs may be any that keep to these rules, and one draw needn't show every extreme that they name: `segments`: in each row, segment numbers never fall and each document's positions are contiguous; every document of a row has 20 or more positions; positions after the row's last document hold 64 (padding). Some row is one document of 2048 tokens, some row ends in padding. `norm_params`: rows 0 and 2 are gains, rows 1 and 3 are biases.
All inputs are finite; a program needn't handle non-finite values.
Results may differ from a plain program's by a relative error of at most 0.023.
Values may be sent and summed in bfloat16 or wider, within the bound.
No kernel may reach another device: no remote copies, remote signals or barrier semaphores. Data moves between devices by JAX's collectives and lax.ppermute only.
A program may use at most 128 MiB of HBM per device.

v0:
```python
import jax
import jax.numpy as jnp
from jax import lax
from jax.sharding import PartitionSpec as P

HEAD_DIM = 64
MAXDOCS = 64
EPSILON = 1e-05
ROPE_BASE = 1000.0
NEGATIVE = -1e30


def layer_norm(total, gain, bias):
    center = jnp.mean(total, axis=-1, keepdims=True)
    shifted = total - center
    spread = jnp.mean(shifted * shifted, axis=-1, keepdims=True)
    return shifted * lax.rsqrt(spread + EPSILON) * gain + bias


def positions_of(segment_row):
    labels = jnp.arange(MAXDOCS + 1, dtype=jnp.int32)
    chosen = segment_row[:, None] == labels[None, :]
    counts = jnp.sum(chosen.astype(jnp.int32), axis=0, dtype=jnp.int32)
    starts = jnp.cumsum(counts, dtype=jnp.int32) - counts
    first = jnp.sum(jnp.where(chosen, starts[None, :], 0), axis=1, dtype=jnp.int32)
    return jnp.arange(segment_row.shape[0], dtype=jnp.int32) - first


def rotary_tables(positions, depth):
    half = depth // 2
    powers = jnp.arange(half, dtype=jnp.float32) * (-2.0 / depth)
    inverse = ROPE_BASE**powers
    angles = positions.astype(jnp.float32)[..., None] * inverse
    return (jnp.cos(angles), jnp.sin(angles))


def rotate(field, cosine, sine):
    half = field.shape[-1] // 2
    first = field[..., :half]
    second = field[..., half:]
    return jnp.concatenate(
        [first * cosine - second * sine, second * cosine + first * sine], axis=-1
    )


def swiglu(gate, up):
    return jax.nn.silu(gate) * up


def block_mask(segment_row, start, block):
    length = segment_row.shape[0]
    own = lax.dynamic_slice_in_dim(segment_row, start, block, 0)
    places = jnp.arange(length, dtype=jnp.int32)
    own_places = start + jnp.arange(block, dtype=jnp.int32)
    same = own[:, None] == segment_row[None, :]
    live = (own[:, None] < MAXDOCS) | (own_places[:, None] == places[None, :])
    return same & live


def block_scores(query_block, keys, allowed, scale):
    scores = (
        jnp.einsum("qhd,khd->hqk", query_block, keys, preferred_element_type=jnp.float32) * scale
    )
    return jnp.where(allowed[None], scores, NEGATIVE)


def attend_row(queries, keys, values, segment_row):
    length, heads, depth = queries.shape
    block = min(512, length)
    scale = depth ** (-0.5)

    def one_block(start):
        query_block = lax.dynamic_slice_in_dim(queries, start, block, 0)
        scores = block_scores(query_block, keys, block_mask(segment_row, start, block), scale)
        highest = jnp.max(scores, axis=-1, keepdims=True)
        expo = jnp.exp(scores - highest)
        total = jnp.sum(expo, axis=-1, keepdims=True)
        probs = (expo / total).astype(jnp.bfloat16)
        mixed = jnp.einsum("hqk,khd->qhd", probs, values, preferred_element_type=jnp.float32)
        return (mixed.astype(jnp.bfloat16), (highest + jnp.log(total))[..., 0])

    starts = jnp.arange(length // block, dtype=jnp.int32) * block
    mixed, logsum = lax.map(one_block, starts)
    return (mixed.reshape(length, heads, depth), logsum)


def attend_back(queries, keys, values, segment_row, logsum, heads_grad):
    length, heads, depth = queries.shape
    block = min(512, length)
    scale = depth ** (-0.5)

    def one_block(carry, inputs):
        start, block_logsum = inputs
        query_block = lax.dynamic_slice_in_dim(queries, start, block, 0)
        grad_block = lax.dynamic_slice_in_dim(heads_grad, start, block, 0)
        scores = block_scores(query_block, keys, block_mask(segment_row, start, block), scale)
        probs = jnp.exp(scores - block_logsum[..., None])
        probs_grad = jnp.einsum(
            "qhd,khd->hqk", grad_block, values, preferred_element_type=jnp.float32
        )
        weighted = jnp.sum(probs * probs_grad, axis=-1, keepdims=True)
        score_low = (probs * (probs_grad - weighted)).astype(jnp.bfloat16)
        query_grad = (
            jnp.einsum("hqk,khd->qhd", score_low, keys, preferred_element_type=jnp.float32) * scale
        )
        key_grad = (
            carry[0]
            + jnp.einsum("hqk,qhd->khd", score_low, query_block, preferred_element_type=jnp.float32)
            * scale
        )
        value_grad = carry[1] + jnp.einsum(
            "hqk,qhd->khd",
            probs.astype(jnp.bfloat16),
            grad_block,
            preferred_element_type=jnp.float32,
        )
        return ((key_grad, value_grad), query_grad)

    starts = jnp.arange(length // block, dtype=jnp.int32) * block
    zeros = jnp.zeros((length, heads, depth), jnp.float32)
    (key_grad, value_grad), query_grad = lax.scan(one_block, (zeros, zeros), (starts, logsum))
    return (query_grad.reshape(length, heads, depth), key_grad, value_grad)


def per_device(
    layer_input,
    segments,
    qkv_weight,
    out_weight,
    gate_weight,
    up_weight,
    down_weight,
    norm_params,
    cotangent,
):
    piece_len, batch_rows, width = layer_input.shape
    seq_len = piece_len * lax.axis_size("tensor")
    head_dim = HEAD_DIM
    local_heads = out_weight.shape[0] // head_dim
    head_cols = local_heads * head_dim
    positions = jax.vmap(positions_of)(segments)
    cosine, sine = rotary_tables(positions, head_dim)
    cosine = cosine[:, :, None, :]
    sine = sine[:, :, None, :]

    def project_heads(gathered):
        joint = jnp.einsum("srd,dc->rsc", gathered, qkv_weight, preferred_element_type=jnp.float32)
        joint = joint.reshape(batch_rows, seq_len, local_heads, 3, head_dim)
        queries = rotate(joint[:, :, :, 0], cosine, sine).astype(jnp.bfloat16)
        keys = rotate(joint[:, :, :, 1], cosine, sine).astype(jnp.bfloat16)
        return (queries, keys, joint[:, :, :, 2].astype(jnp.bfloat16))

    def feed_forward(gathered):
        gate = jnp.einsum("srd,df->srf", gathered, gate_weight, preferred_element_type=jnp.float32)
        up = jnp.einsum("srd,df->srf", gathered, up_weight, preferred_element_type=jnp.float32)
        return (gate, up)

    gathered_input = lax.all_gather(layer_input, "tensor", axis=0, tiled=True)
    queries, keys, values = project_heads(gathered_input)
    heads_out, logsum = lax.map(lambda parts: attend_row(*parts), (queries, keys, values, segments))
    heads_flat = heads_out.reshape(batch_rows, seq_len, head_cols)
    used = heads_flat
    attention = lax.psum_scatter(
        jnp.einsum("rsc,cd->srd", used, out_weight, preferred_element_type=jnp.float32).astype(
            jnp.bfloat16
        ),
        "tensor",
        scatter_dimension=0,
        tiled=True,
    ).astype(jnp.float32)
    normed, first_pull = jax.vjp(
        layer_norm, layer_input.astype(jnp.float32) + attention, norm_params[0], norm_params[1]
    )
    gathered_norm = lax.all_gather(normed.astype(jnp.bfloat16), "tensor", axis=0, tiled=True)
    gate, up = feed_forward(gathered_norm)
    hidden = swiglu(gate, up).astype(jnp.bfloat16)
    used = hidden
    branch = lax.psum_scatter(
        jnp.einsum("srf,fd->srd", used, down_weight, preferred_element_type=jnp.float32).astype(
            jnp.bfloat16
        ),
        "tensor",
        scatter_dimension=0,
        tiled=True,
    ).astype(jnp.float32)
    output, second_pull = jax.vjp(layer_norm, normed + branch, norm_params[2], norm_params[3])
    second_grad, gain_two, bias_two = second_pull(cotangent.astype(jnp.float32))
    gate_again, up_again = feed_forward(gathered_norm)
    piece = lax.all_gather(second_grad.astype(jnp.bfloat16), "tensor", axis=0, tiled=True)
    rows_grad = jnp.einsum("srd,fd->srf", piece, down_weight, preferred_element_type=jnp.float32)
    hidden_grad = rows_grad
    used = hidden
    down_part = jnp.einsum("srf,srd->fd", used, piece, preferred_element_type=jnp.float32)
    hidden_grad, down_part = (hidden_grad, down_part)
    unused, swiglu_pull = jax.vjp(swiglu, gate_again, up_again)
    gate_full, up_full = swiglu_pull(hidden_grad)
    gate_low = gate_full.astype(jnp.bfloat16)
    up_low = up_full.astype(jnp.bfloat16)
    gate_part = jnp.einsum(
        "srd,srf->df", gathered_norm, gate_low, preferred_element_type=jnp.float32
    )
    up_part = jnp.einsum("srd,srf->df", gathered_norm, up_low, preferred_element_type=jnp.float32)
    term = jnp.einsum("srf,df->srd", gate_low, gate_weight, preferred_element_type=jnp.float32)
    normed_grad = second_grad + lax.psum_scatter(
        (
            term + jnp.einsum("srf,df->srd", up_low, up_weight, preferred_element_type=jnp.float32)
        ).astype(jnp.bfloat16),
        "tensor",
        scatter_dimension=0,
        tiled=True,
    ).astype(jnp.float32)
    first_grad, gain_one, bias_one = first_pull(normed_grad)
    query_again, key_again, value_again = project_heads(gathered_input)
    piece = lax.all_gather(first_grad.astype(jnp.bfloat16), "tensor", axis=0, tiled=True)
    rows_grad = jnp.einsum("srd,cd->rsc", piece, out_weight, preferred_element_type=jnp.float32)
    heads_grad = rows_grad
    used = heads_flat
    out_part = jnp.einsum("rsc,srd->cd", used, piece, preferred_element_type=jnp.float32)
    heads_grad, out_part = (heads_grad, out_part)
    heads_low = heads_grad.astype(jnp.bfloat16).reshape(batch_rows, seq_len, local_heads, head_dim)
    query_grad, key_grad, value_grad = lax.map(
        lambda parts: attend_back(*parts),
        (query_again, key_again, value_again, segments, logsum, heads_low),
    )
    query_raw = rotate(query_grad, cosine, -sine)
    key_raw = rotate(key_grad, cosine, -sine)
    joint_grad = (
        jnp.stack([query_raw, key_raw, value_grad], axis=3)
        .reshape(batch_rows, seq_len, 3 * head_cols)
        .astype(jnp.bfloat16)
    )
    qkv_part = jnp.einsum(
        "srd,rsc->dc", gathered_input, joint_grad, preferred_element_type=jnp.float32
    )
    used = joint_grad
    input_grad = first_grad + lax.psum_scatter(
        jnp.einsum("rsc,dc->srd", used, qkv_weight, preferred_element_type=jnp.float32).astype(
            jnp.bfloat16
        ),
        "tensor",
        scatter_dimension=0,
        tiled=True,
    ).astype(jnp.float32)
    qkv_grad, out_grad, gate_grad, up_grad, down_grad = lax.psum(
        (qkv_part, out_part, gate_part, up_part, down_part), "dp"
    )
    norm_grads = lax.psum(
        jnp.stack([gain_one, bias_one, gain_two, bias_two], axis=0), ("dp", "tensor")
    )
    return (
        output.astype(jnp.bfloat16),
        input_grad,
        qkv_grad,
        out_grad,
        gate_grad,
        up_grad,
        down_grad,
        norm_grads,
    )


def solution(mesh):
    placed = (
        P("tensor", "dp", None),
        P("dp", None),
        P(None, "tensor"),
        P("tensor", None),
        P(None, "tensor"),
        P(None, "tensor"),
        P("tensor", None),
        P(),
        P("tensor", "dp", None),
    )
    return jax.shard_map(
        per_device,
        mesh=mesh,
        in_specs=placed,
        out_specs=(
            P("tensor", "dp", None),
            P("tensor", "dp", None),
            P(None, "tensor"),
            P("tensor", None),
            P(None, "tensor"),
            P(None, "tensor"),
            P("tensor", None),
            P(),
        ),
        check_vma=False,
    )
```

profile of v0, /device:TPU:0, one launch (start us, length us, event | category | flops | bytes accessed | tf_op | source)
XLA Modules:
  0.0 1039.7 jit_solution(2395580110291607030)
XLA Ops:
  13.4 62.3 %all-gather.5.cloned.1.call-done = bf16[2048,1,768]{2,0,1:T(8,128)(2,1)} async-done(((bf16[512,1,768]{2,0,1:T(8,128)(2,1)}), bf16[2048,1,768]{2,0,1:T(8,128)(2,1)}) %all-gather.5.cloned.1.call-update) | async-done | bytes 3145744 | tf_op jit(solution)/shard_map/all_gather | solution.py:158
  75.8 4.2 fusion.62
  82.3 105.2 %while.47 = (s32[]{:T(128)}, bf16[4,512,3,64]{1,3,2,0:T(8,128)(2,1)}, f32[4,3,512]{2,1,0:T(4,128)}, s32[4]{0:T(128)S(1)}, s32[2048]{0:T(1024)S(1)}, /*index=5*/b...) while((s32[]{:T(128)}, ...), condition=%wide.region_6.7_spmd, body=%wide.region_3.6_spmd.sunk | while | flops 847347200 | bytes 43979956 | solution.py:83
  87.0 6.9 fusion.148
  93.9 6.8 fusion.149
  100.6 7.3 fusion.150
  113.3 6.9 fusion.148
  120.2 6.8 fusion.149
  126.9 7.3 fusion.150
  139.5 6.9 fusion.148
  146.5 6.8 fusion.149
  153.2 7.3 fusion.150
  165.8 6.9 fusion.148
  172.7 6.8 fusion.149
  179.5 7.3 fusion.150
  194.5 57.7 %reduce-scatter.5.cloned.1.call-done = bf16[512,1,768]{2,0,1:T(8,128)(2,1)} async-done(((bf16[2048,1,768]{2,0,1:T(8,128)(2,1)}), bf16[512,1,768]{2,0,1:T(8,128)(2,1)}) %reduce-scatter.5.cloned.1.call-update) | async-done | bytes 786448 | tf_op jit(solution)/shard_map/reduce_scatter | solution.py:163
  258.1 63.2 %all-gather.7.cloned.1.call-done = bf16[2048,1,768]{2,0,1:T(8,128)(2,1)} async-done(((bf16[512,1,768]{2,0,1:T(8,128)(2,1)}), bf16[2048,1,768]{2,0,1:T(8,128)(2,1)}) %all-gather.7.cloned.1.call-update) | async-done | bytes 3145744 | tf_op jit(solution)/shard_map/all_gather | solution.py:174
  321.3 5.0 fusion.58
  326.4 5.0 multiply_convert_fusion.2
  333.0 4.0 fusion.65
  337.1 59.2 %reduce-scatter.7.cloned.1.call-done = bf16[512,1,768]{2,0,1:T(8,128)(2,1)} async-done(((bf16[2048,1,768]{2,0,1:T(8,128)(2,1)}), bf16[512,1,768]{2,0,1:T(8,128)(2,1)}) %reduce-scatter.7.cloned.1.call-update) | async-done | bytes 786448 | tf_op jit(solution)/shard_map/reduce_scatter | solution.py:178
  403.8 63.5 %all-gather.9.cloned.1.call-done = bf16[2048,1,768]{2,0,1:T(8,128)(2,1)} async-done(((bf16[512,1,768]{2,0,1:T(8,128)(2,1)}), bf16[2048,1,768]{2,0,1:T(8,128)(2,1)}) %all-gather.9.cloned.1.call-update) | async-done | bytes 3145744 | tf_op jit(solution)/shard_map/all_gather | solution.py:189
  467.3 9.5 multiply_convert_fusion.1
  479.5 4.0 fusion.66
  483.6 59.1 %reduce-scatter.9.cloned.1.call-done = bf16[512,1,768]{2,0,1:T(8,128)(2,1)} async-done(((bf16[2048,1,768]{2,0,1:T(8,128)(2,1)}), bf16[512,1,768]{2,0,1:T(8,128)(2,1)}) %reduce-scatter.9.cloned.1.call-update) | async-done | bytes 786448 | tf_op jit(solution)/shard_map/reduce_scatter | solution.py:204
  542.8 3.3 multiply_reduce_fusion.1
  549.5 63.4 %all-gather.11.cloned.1.call-done = bf16[2048,1,768]{2,0,1:T(8,128)(2,1)} async-done(((bf16[512,1,768]{2,0,1:T(8,128)(2,1)}), bf16[2048,1,768]{2,0,1:T(8,128)(2,1)}) %all-gather.11.cloned.1.call-update) | async-done | bytes 3145744 | tf_op jit(solution)/shard_map/all_gather | solution.py:214
  613.0 4.0 fusion.68
  616.9 191.6 %while.48 = (s32[]{:T(128)}, f32[2048,3,64]{0,2,1:T(8,128)}, f32[2048,3,64]{0,2,1:T(8,128)}, f32[4,512,3,64]{1,0,3,2:T(4,128)}, s32[4]{0:T(128)S(1)}, /*index=5*...) while((s32[]{:T(128)}, f32[2048,3,64]{0,2,1:T(8,128)}, ...), condition=%wide.region_20.21_spmd.clone, body=%wide.region_18.20_spmd.clone.sunk | while | flops 2066710016 | bytes 151975328 | solution.py:121
  632.8 3.2 fusion.160
  636.1 5.7 fusion.163
  641.7 6.1 multiply_reduce_fusion.6
  647.9 6.1 multiply_convert_fusion.4
  654.0 5.1 fusion.164
  659.1 3.5 fusion.162
  663.1 8.6 dynamic_update_slice.33
  677.2 3.2 fusion.160
  680.5 6.3 fusion.163
  686.8 6.1 multiply_reduce_fusion.6
  692.9 6.1 multiply_convert_fusion.4
  699.0 5.1 fusion.164
  704.2 4.1 fusion.162
  708.7 8.6 dynamic_update_slice.33
  722.9 3.2 fusion.160
  726.1 6.3 fusion.163
  732.4 6.1 multiply_reduce_fusion.6
  738.5 6.1 multiply_convert_fusion.4
  744.6 5.1 fusion.164
  749.8 4.1 fusion.162
  754.3 8.6 dynamic_update_slice.33
  768.5 3.1 fusion.160
  771.6 6.3 fusion.163
  777.8 6.1 multiply_reduce_fusion.6
  784.0 6.1 multiply_convert_fusion.4
  790.1 5.1 fusion.164
  795.2 4.1 fusion.162
  799.7 8.6 dynamic_update_slice.33
  815.6 4.0 fusion.67
  819.7 7.1 fusion.48
  826.8 4.2 fusion.52
  831.0 4.2 fusion.54
  837.3 3.2 fusion.75
  841.3 42.9 %psum.47 = f32[4,768]{1,0:T(4,128)} all-reduce(f32[4,768]{1,0:T(4,128)S(1)} %pad_maximum_fusion.2), channel_id=1, replica_groups=mesh['dp'=8,'tensor'=4] {'dp','tensor'}, use_global_device_ids=true, to_apply=%region_31.32 | all-reduce | flops 3072 | bytes 24576 | tf_op jit(solution)/shard_map/psum | solution.py:247
  888.4 134.1 %all-reduce.3.cloned.1.call-done = (f32[768,576]{0,1:T(8,128)}, f32[192,768]{1,0:T(8,128)}, f32[768,768]{1,0:T(8,128)}, f32[768,768]{1,0:T(8,128)}, f32[768,768]{1,0:T(8,128)}) async-done(((f32[768,576]{0,1:T(8,128)}, f32[192,768]{1,0:T(8,128)}, f32[768,768]{1,0:T(8,128)}, f32[768,768]{1,0:T(8,128)}, f32[768,768]{1,0:T(8,128)}), (f32[768,576]{0,1:T(8,128)}, f32[192,768]{1,0:T(8,128)}, f32[768,768]{1,0:T(8,128)}, ...) | async-done | bytes 9437200 | tf_op jit(solution)/shard_map/psum | solution.py:244
  (282 shorter events, 90.1 us)
Async XLA Ops:
  7.2 325.9 %copy-start = (bf16[768,768]{1,0:T(8,128)(2,1)S(1)}, bf16[768,768]{1,0:T(8,128)(2,1)}, u32[]{:S(2)}) copy-start(bf16[768,768]{1,0:T(8,128)(2,1)} %param.19) | copy-start | bytes 3538948
  7.2 68.6 %all-gather.5.cloned.1.call-start = ((), (), s32[]{:S(2)}) async-start(), calls=%async_computation.4 | async-start | bytes 3932160 | tf_op jit(solution)/shard_map/all_gather | solution.py:158
  7.9 244.3 %reduce-scatter.5.cloned.1.call-start = ((), (), s32[]{:S(2)}) async-start(), calls=%async_computation.5 | async-start | bytes 3932160 | tf_op jit(solution)/shard_map/reduce_scatter | solution.py:163
  13.4 67.3 %copy-start.21 = (f32[2048,32]{0,1:T(8,128)}, f32[2048,32]{0,1:T(8,128)S(1)}, u32[]{:S(2)}) copy-start(f32[2048,32]{0,1:T(8,128)S(1)} %get-tuple-element.312) | copy-start | bytes 786436
  187.4 5.5 copy-start.52
  187.4 2.8 copy-start.50
  193.0 59.2 %copy-start.9 = (bf16[512,1,768]{2,0,1:T(8,128)(2,1)S(1)}, bf16[512,1,768]{2,0,1:T(8,128)(2,1)}, u32[]{:S(2)}) copy-start(bf16[512,1,768]{2,0,1:T(8,128)(2,1)} %param.13) | copy-start | bytes 2359300
  193.0 128.3 %all-gather.7.cloned.1.call-start = ((), (), s32[]{:S(2)}) async-start(), calls=%async_computation.6 | async-start | bytes 3932160 | tf_op jit(solution)/shard_map/all_gather | solution.py:174
  252.2 4.2 copy-start.10
  252.2 4.2 copy-start.31
  257.8 138.5 %reduce-scatter.7.cloned.1.call-start = ((), (), s32[]{:S(2)}) async-start(), calls=%async_computation.7 | async-start | bytes 3932160 | tf_op jit(solution)/shard_map/reduce_scatter | solution.py:178
  321.3 5.1 copy-start.44
  321.3 5.1 copy-start.47
  326.4 5.0 copy-start.59
  337.1 130.2 %all-gather.9.cloned.1.call-start = ((), (), s32[]{:S(2)}) async-start(), calls=%async_computation.8 | async-start | bytes 3932160 | tf_op jit(solution)/shard_map/all_gather | solution.py:189
  403.8 139.0 %reduce-scatter.9.cloned.1.call-start = ((), (), s32[]{:S(2)}) async-start(), calls=%async_computation.9 | async-start | bytes 3932160 | tf_op jit(solution)/shard_map/reduce_scatter | solution.py:204
  467.3 9.5 copy-start.46
  476.8 2.7 copy-start.55
  483.5 59.2 %copy-start.11 = (bf16[512,1,768]{2,0,1:T(8,128)(2,1)S(1)}, bf16[512,1,768]{2,0,1:T(8,128)(2,1)}, u32[]{:S(2)}) copy-start(bf16[512,1,768]{2,0,1:T(8,128)(2,1)} %reduce-scatter.5.cloned.1.call-done) | copy-start | bytes 2359300
  483.5 59.2 %copy-start.29 = (f32[512]{0:T(512)S(1)}, f32[512]{0:T(512)}, u32[]{:S(2)}) copy-start(f32[512]{0:T(512)} %copy-done.28) | copy-start | bytes 6148
  483.5 59.2 %copy-start.33 = (f32[512]{0:T(512)S(1)}, f32[512]{0:T(512)}, u32[]{:S(2)}) copy-start(f32[512]{0:T(512)} %copy-done.32) | copy-start | bytes 6148
  483.6 62.6 %copy-start.37 = (f32[512]{0:T(512)S(1)}, f32[512]{0:T(512)}, u32[]{:S(2)}) copy-start(f32[512]{0:T(512)} %copy-done.36) | copy-start | bytes 6148
  483.6 129.4 %all-gather.11.cloned.1.call-start = ((), (), s32[]{:S(2)}) async-start(), calls=%async_computation.10 | async-start | bytes 3932160 | tf_op jit(solution)/shard_map/all_gather | solution.py:214
  542.8 3.4 copy-start.13
  542.8 3.4 copy-start.20
  547.2 65.8 %copy-start.51 = (bf16[192,768]{1,0:T(8,128)(2,1)S(1)}, bf16[192,768]{1,0:T(8,128)(2,1)}, u32[]{:S(2)}) copy-start(bf16[192,768]{1,0:T(8,128)(2,1)} %param.16) | copy-start | bytes 884740
  547.2 69.7 %copy-start.34 = (f32[512]{0:T(512)}, f32[512]{0:T(512)S(1)}, u32[]{:S(2)}) copy-start(f32[512]{0:T(512)S(1)} %negate_multiply_fusion) | copy-start | bytes 6148
  549.5 334.8 %reduce-scatter.11.cloned.1.call-start = ((), (), s32[]{:S(2)}) async-start(), calls=%async_computation.11 | async-start | bytes 3932160 | tf_op jit(solution)/shard_map/reduce_scatter | solution.py:236
  549.5 67.4 %copy-start.53 = (s32[4]{0:T(128)S(1)}, s32[4]{0:T(128)}, u32[]{:S(2)}) copy-start(s32[4]{0:T(128)} %copy-done.52) | copy-start | bytes 52
  627.3 8.7 copy-start.4
  627.3 8.7 copy-start.7
  632.8 3.2 copy-start.3
  654.0 5.1 copy-start.2
  659.1 12.6 %copy-start.5 = (bf16[2048,3,64]{0,2,1:T(8,128)(2,1)S(1)}, bf16[2048,3,64]{0,2,1:T(8,128)(2,1)}, u32[]{:S(2)}) copy-start(bf16[2048,3,64]{0,2,1:T(8,128)(2,1)} %copy-done.4) | copy-start | bytes 2359300 | tf_op jit(solution)/shard_map/while/body/eval_jaxpr/while
  659.1 12.6 %copy-start.8 = (bf16[2048,3,64]{0,2,1:T(8,128)(2,1)S(1)}, bf16[2048,3,64]{0,2,1:T(8,128)(2,1)}, u32[]{:S(2)}) copy-start(bf16[2048,3,64]{0,2,1:T(8,128)(2,1)} %copy-done.7) | copy-start | bytes 2359300 | tf_op jit(solution)/shard_map/while/body/eval_jaxpr/while
  671.7 8.7 copy-start.4
  671.7 8.7 copy-start.7
  677.2 3.2 copy-start.3
  699.0 5.1 copy-start.2
  704.1 13.2 %copy-start.5 = (bf16[2048,3,64]{0,2,1:T(8,128)(2,1)S(1)}, bf16[2048,3,64]{0,2,1:T(8,128)(2,1)}, u32[]{:S(2)}) copy-start(bf16[2048,3,64]{0,2,1:T(8,128)(2,1)} %copy-done.4) | copy-start | bytes 2359300 | tf_op jit(solution)/shard_map/while/body/eval_jaxpr/while
  704.2 13.2 %copy-start.8 = (bf16[2048,3,64]{0,2,1:T(8,128)(2,1)S(1)}, bf16[2048,3,64]{0,2,1:T(8,128)(2,1)}, u32[]{:S(2)}) copy-start(bf16[2048,3,64]{0,2,1:T(8,128)(2,1)} %copy-done.7) | copy-start | bytes 2359300 | tf_op jit(solution)/shard_map/while/body/eval_jaxpr/while
  717.3 8.7 copy-start.4
  717.3 8.7 copy-start.7
  722.8 3.2 copy-start.3
  744.6 5.1 copy-start.2
  749.7 13.2 %copy-start.5 = (bf16[2048,3,64]{0,2,1:T(8,128)(2,1)S(1)}, bf16[2048,3,64]{0,2,1:T(8,128)(2,1)}, u32[]{:S(2)}) copy-start(bf16[2048,3,64]{0,2,1:T(8,128)(2,1)} %copy-done.4) | copy-start | bytes 2359300 | tf_op jit(solution)/shard_map/while/body/eval_jaxpr/while
  749.8 13.2 %copy-start.8 = (bf16[2048,3,64]{0,2,1:T(8,128)(2,1)S(1)}, bf16[2048,3,64]{0,2,1:T(8,128)(2,1)}, u32[]{:S(2)}) copy-start(bf16[2048,3,64]{0,2,1:T(8,128)(2,1)} %copy-done.7) | copy-start | bytes 2359300 | tf_op jit(solution)/shard_map/while/body/eval_jaxpr/while
  762.9 8.6 copy-start.4
  762.9 8.6 copy-start.7
  768.4 3.1 copy-start.3
  790.1 5.1 copy-start.2
  795.2 13.2 %copy-start.5 = (bf16[2048,3,64]{0,2,1:T(8,128)(2,1)S(1)}, bf16[2048,3,64]{0,2,1:T(8,128)(2,1)}, u32[]{:S(2)}) copy-start(bf16[2048,3,64]{0,2,1:T(8,128)(2,1)} %copy-done.4) | copy-start | bytes 2359300 | tf_op jit(solution)/shard_map/while/body/eval_jaxpr/while
  795.2 13.1 %copy-start.8 = (bf16[2048,3,64]{0,2,1:T(8,128)(2,1)S(1)}, bf16[2048,3,64]{0,2,1:T(8,128)(2,1)}, u32[]{:S(2)}) copy-start(bf16[2048,3,64]{0,2,1:T(8,128)(2,1)} %copy-done.7) | copy-start | bytes 2359300 | tf_op jit(solution)/shard_map/while/body/eval_jaxpr/while
  819.7 202.8 %all-reduce.3.cloned.1.call-start = ((), (), s32[]{:S(2)}) async-start(), calls=%async_computation.12 | async-start | bytes 18874368 | tf_op jit(solution)/shard_map/psum | solution.py:244
  819.7 7.1 copy-start.45
  819.7 7.1 copy-start.58
  826.8 4.2 copy-start.56
  831.0 4.2 copy-start.16
  831.0 4.2 copy-start.19
  840.6 43.7 %copy-start.15 = (f32[512,1,768]{2,0,1:T(8,128)S(1)}, f32[512,1,768]{2,0,1:T(8,128)}, u32[]{:S(2)}) copy-start(f32[512,1,768]{2,0,1:T(8,128)} %copy-done.14) | copy-start | bytes 4718596
  840.6 43.7 %copy-start.35 = (f32[512]{0:T(512)S(1)}, f32[512]{0:T(512)}, u32[]{:S(2)}) copy-start(f32[512]{0:T(512)} %copy-done.34) | copy-start | bytes 6148
  1022.5 3.0 copy-start.27
  1022.5 3.8 copy-start.25
  1028.8 3.9 copy-start.1
  (23 other events, 36.4 us)
Sparse Core Ops, SparseCore 0:
  9.6 66.1 all-gather.4
  193.1 59.0 reduce-scatter.4
  257.9 63.3 all-gather.6
  337.2 59.0 reduce-scatter.6
  403.9 63.3 all-gather.8
  483.7 59.0 reduce-scatter.8
  549.6 63.3 all-gather.10
  819.8 59.9 reduce-scatter.10
  884.7 137.7 all-reduce.2
where the time goes:
time: 1050 us; the launch traced here: 1040 us
  waiting for transfers between devices  563 us (54%)
  matrix products  220 us (21%)
  other arithmetic  98.6 us (9%)
  local copies, waits for them, and re-layouts  72.4 us (7%)
  blocking collectives  42.9 us (4%)
  loops' own time  26.6 us (3%)
  between operations  14.9 us (1%)
    psum x1, waiting for transfers between devices, per_device(): lax.psum((qkv_part, out_part, gate_part, up_part, down_part), 'dp')  134 us
    all_gather x1, waiting for transfers between devices, per_device(): lax.all_gather(second_grad.astype(jnp.bfloat16), 'tensor', axis=0, tiled=...  63.5 us
    all_gather x1, waiting for transfers between devices, per_device(): lax.all_gather(first_grad.astype(jnp.bfloat16), 'tensor', axis=0, tiled=T...  63.4 us
    all_gather x1, waiting for transfers between devices, per_device(): lax.all_gather(normed.astype(jnp.bfloat16), 'tensor', axis=0, tiled=True)  63.2 us
    all_gather x1, waiting for transfers between devices, per_device(): gathered_input = lax.all_gather(layer_input, 'tensor', axis=0, tiled=True)  62.3 us
    reduce_scatter x1, waiting for transfers between devices, per_device(): lax.psum_scatter(jnp.einsum('srf,fd->srd', used, down_weight, preferred_e...  59.2 us
    reduce_scatter x1, waiting for transfers between devices, per_device(): lax.psum_scatter((term + jnp.einsum('srf,df->srd', up_low, up_weight, pre...  59.1 us
    reduce_scatter x1, waiting for transfers between devices, per_device(): lax.psum_scatter(jnp.einsum('rsc,cd->srd', used, out_weight, preferred_el...  57.7 us
  transfers between devices with their start and end apart: 9, of which 8 were waited for; matrix products, arithmetic and copies ran while one was open for 3% of the time, Pallas kernels for 0%

commit v1 on v0

--- a/solution.py
+++ b/solution.py
@@ -244,8 +244,11 @@
     qkv_grad, out_grad, gate_grad, up_grad, down_grad = lax.psum(
         (qkv_part, out_part, gate_part, up_part, down_part), "dp"
     )
-    norm_grads = lax.psum(
-        jnp.stack([gain_one, bias_one, gain_two, bias_two], axis=0), ("dp", "tensor")
+    norm_grads = jnp.sum(
+        lax.all_gather(
+            jnp.stack([gain_one, bias_one, gain_two, bias_two], axis=0), ("dp", "tensor")
+        ),
+        axis=0,
     )
     return (
         output.astype(jnp.bfloat16),

time: 1050 us -> 1060 us (level)
  blocking collectives: 42.9 us -> 73.9 us
  waiting for transfers between devices: 563 us -> 536 us
    all_gather x0 -> x1, blocking collectives: none -> 73.9 us  [per_device(): lax.all_gather(jnp.stack([gain_one, bias_one, gain_two, bias_two], axis=0...]
    psum x1 -> x0, blocking collectives: 42.9 us -> none  [per_device(): lax.psum(jnp.stack([gain_one, bias_one, gain_two, bias_two], axis=0), ('d...]
    psum x1, waiting for transfers between devices: 134 us -> 106 us  [per_device(): lax.psum((qkv_part, out_part, gate_part, up_part, down_part), 'dp')]
where the time goes in v1:
time: 1060 us; the launch traced here: 1040 us
  waiting for transfers between devices  536 us (51%)
  matrix products  220 us (21%)
  other arithmetic  99.3 us (9%)
  blocking collectives  73.9 us (7%)
  local copies, waits for them, and re-layouts  72.4 us (7%)
  loops' own time  26.6 us (3%)
  between operations  14.9 us (1%)
    psum x1, waiting for transfers between devices, per_device(): lax.psum((qkv_part, out_part, gate_part, up_part, down_part), 'dp')  106 us
    all_gather x1, blocking collectives, per_device(): lax.all_gather(jnp.stack([gain_one, bias_one, gain_two, bias_two], axis=0...  73.9 us
    all_gather x1, waiting for transfers between devices, per_device(): lax.all_gather(second_grad.astype(jnp.bfloat16), 'tensor', axis=0, tiled=...  63.5 us
    all_gather x1, waiting for transfers between devices, per_device(): lax.all_gather(first_grad.astype(jnp.bfloat16), 'tensor', axis=0, tiled=T...  63.4 us
    all_gather x1, waiting for transfers between devices, per_device(): lax.all_gather(normed.astype(jnp.bfloat16), 'tensor', axis=0, tiled=True)  63.2 us
    all_gather x1, waiting for transfers between devices, per_device(): gathered_input = lax.all_gather(layer_input, 'tensor', axis=0, tiled=True)  62.3 us
    reduce_scatter x1, waiting for transfers between devices, per_device(): lax.psum_scatter(jnp.einsum('srf,fd->srd', used, down_weight, preferred_e...  59.2 us
    reduce_scatter x1, waiting for transfers between devices, per_device(): lax.psum_scatter((term + jnp.einsum('srf,df->srd', up_low, up_weight, pre...  59.1 us
  transfers between devices with their start and end apart: 9, of which 8 were waited for; matrix products, arithmetic and copies ran while one was open for 3% of the time, Pallas kernels for 0%

profile of v1, /device:TPU:0, one launch (start us, length us, event | category | flops | bytes accessed | tf_op | source)
XLA Modules:
  0.0 1043.6 jit_solution(17039508712609658091)
XLA Ops:
  13.4 62.3 %all-gather.7.cloned.1.call-done = bf16[2048,1,768]{2,0,1:T(8,128)(2,1)} async-done(((bf16[512,1,768]{2,0,1:T(8,128)(2,1)}), bf16[2048,1,768]{2,0,1:T(8,128)(2,1)}) %all-gather.7.cloned.1.call-update) | async-done | bytes 3145744 | tf_op jit(solution)/shard_map/all_gather | solution.py:158
  75.8 4.2 fusion.62
  82.3 105.2 %while.47 = (s32[]{:T(128)}, bf16[4,512,3,64]{1,3,2,0:T(8,128)(2,1)}, f32[4,3,512]{2,1,0:T(4,128)}, s32[4]{0:T(128)S(1)}, s32[2048]{0:T(1024)S(1)}, /*index=5*/b...) while((s32[]{:T(128)}, ...), condition=%wide.region_6.7_spmd, body=%wide.region_3.6_spmd.sunk | while | flops 847347200 | bytes 43979956 | solution.py:83
  87.0 6.9 fusion.148
  93.9 6.8 fusion.149
  100.6 7.3 fusion.150
  113.3 6.9 fusion.148
  120.2 6.8 fusion.149
  126.9 7.3 fusion.150
  139.5 6.9 fusion.148
  146.5 6.8 fusion.149
  153.2 7.3 fusion.150
  165.8 6.9 fusion.148
  172.7 6.8 fusion.149
  179.5 7.3 fusion.150
  194.5 57.7 %reduce-scatter.5.cloned.1.call-done = bf16[512,1,768]{2,0,1:T(8,128)(2,1)} async-done(((bf16[2048,1,768]{2,0,1:T(8,128)(2,1)}), bf16[512,1,768]{2,0,1:T(8,128)(2,1)}) %reduce-scatter.5.cloned.1.call-update) | async-done | bytes 786448 | tf_op jit(solution)/shard_map/reduce_scatter | solution.py:163
  258.1 63.2 %all-gather.9.cloned.1.call-done = bf16[2048,1,768]{2,0,1:T(8,128)(2,1)} async-done(((bf16[512,1,768]{2,0,1:T(8,128)(2,1)}), bf16[2048,1,768]{2,0,1:T(8,128)(2,1)}) %all-gather.9.cloned.1.call-update) | async-done | bytes 3145744 | tf_op jit(solution)/shard_map/all_gather | solution.py:174
  321.3 5.0 fusion.58
  326.4 5.0 multiply_convert_fusion.2
  333.0 4.0 fusion.65
  337.1 59.2 %reduce-scatter.7.cloned.1.call-done = bf16[512,1,768]{2,0,1:T(8,128)(2,1)} async-done(((bf16[2048,1,768]{2,0,1:T(8,128)(2,1)}), bf16[512,1,768]{2,0,1:T(8,128)(2,1)}) %reduce-scatter.7.cloned.1.call-update) | async-done | bytes 786448 | tf_op jit(solution)/shard_map/reduce_scatter | solution.py:178
  403.8 63.5 %all-gather.11.cloned.1.call-done = bf16[2048,1,768]{2,0,1:T(8,128)(2,1)} async-done(((bf16[512,1,768]{2,0,1:T(8,128)(2,1)}), bf16[2048,1,768]{2,0,1:T(8,128)(2,1)}) %all-gather.11.cloned.1.call-update) | async-done | bytes 3145744 | tf_op jit(solution)/shard_map/all_gather | solution.py:189
  467.3 9.5 multiply_convert_fusion.1
  479.5 4.0 fusion.66
  483.6 59.1 %reduce-scatter.9.cloned.1.call-done = bf16[512,1,768]{2,0,1:T(8,128)(2,1)} async-done(((bf16[2048,1,768]{2,0,1:T(8,128)(2,1)}), bf16[512,1,768]{2,0,1:T(8,128)(2,1)}) %reduce-scatter.9.cloned.1.call-update) | async-done | bytes 786448 | tf_op jit(solution)/shard_map/reduce_scatter | solution.py:204
  542.8 3.3 multiply_reduce_fusion.1
  549.5 63.4 %all-gather.13.cloned.1.call-done = bf16[2048,1,768]{2,0,1:T(8,128)(2,1)} async-done(((bf16[512,1,768]{2,0,1:T(8,128)(2,1)}), bf16[2048,1,768]{2,0,1:T(8,128)(2,1)}) %all-gather.13.cloned.1.call-update) | async-done | bytes 3145744 | tf_op jit(solution)/shard_map/all_gather | solution.py:214
  613.0 4.0 fusion.68
  616.9 191.6 %while.48 = (s32[]{:T(128)}, f32[2048,3,64]{0,2,1:T(8,128)}, f32[2048,3,64]{0,2,1:T(8,128)}, f32[4,512,3,64]{1,0,3,2:T(4,128)}, s32[4]{0:T(128)S(1)}, /*index=5*...) while((s32[]{:T(128)}, f32[2048,3,64]{0,2,1:T(8,128)}, ...), condition=%wide.region_20.21_spmd.clone, body=%wide.region_18.20_spmd.clone.sunk | while | flops 2066710016 | bytes 151975328 | solution.py:121
  632.8 3.2 fusion.160
  636.1 5.7 fusion.163
  641.7 6.1 multiply_reduce_fusion.6
  647.9 6.1 multiply_convert_fusion.4
  654.0 5.1 fusion.164
  659.1 3.5 fusion.162
  663.1 8.6 dynamic_update_slice.33
  677.2 3.2 fusion.160
  680.5 6.3 fusion.163
  686.8 6.1 multiply_reduce_fusion.6
  692.9 6.1 multiply_convert_fusion.4
  699.0 5.1 fusion.164
  704.2 4.1 fusion.162
  708.7 8.6 dynamic_update_slice.33
  722.9 3.2 fusion.160
  726.1 6.3 fusion.163
  732.4 6.1 multiply_reduce_fusion.6
  738.5 6.1 multiply_convert_fusion.4
  744.6 5.1 fusion.164
  749.8 4.1 fusion.162
  754.3 8.6 dynamic_update_slice.33
  768.5 3.1 fusion.160
  771.6 6.3 fusion.163
  777.8 6.1 multiply_reduce_fusion.6
  784.0 6.1 multiply_convert_fusion.4
  790.1 5.1 fusion.164
  795.2 4.1 fusion.162
  799.7 8.6 dynamic_update_slice.33
  815.6 4.0 fusion.67
  819.7 7.1 fusion.48
  826.8 4.2 fusion.52
  831.0 4.2 fusion.54
  837.3 3.2 fusion.75
  841.3 73.9 %all-gather.1 = f32[32,4,768]{2,1,0:T(4,128)S(1)} all-gather(f32[1,4,768]{2,1,0:T(4,128)S(1)} %maximum_bitcast_fusion.2), channel_id=2, replica_groups=mesh['dp'=8,'tensor'=4] {'dp','tensor'}, dimensions={0}, use_global_device_ids=true | all-gather | bytes 405504 | tf_op jit(solution)/shard_map/all_gather | solution.py:248
  920.0 106.4 %all-reduce.3.cloned.1.call-done = (f32[768,576]{0,1:T(8,128)}, f32[192,768]{1,0:T(8,128)}, f32[768,768]{1,0:T(8,128)}, f32[768,768]{1,0:T(8,128)}, f32[768,768]{1,0:T(8,128)}) async-done(((f32[768,576]{0,1:T(8,128)}, f32[192,768]{1,0:T(8,128)}, f32[768,768]{1,0:T(8,128)}, f32[768,768]{1,0:T(8,128)}, f32[768,768]{1,0:T(8,128)}), (f32[768,576]{0,1:T(8,128)}, f32[192,768]{1,0:T(8,128)}, f32[768,768]{1,0:T(8,128)}, ...) | async-done | bytes 9437200 | tf_op jit(solution)/shard_map/psum | solution.py:244
  (283 shorter events, 90.8 us)
Async XLA Ops:
  7.2 325.9 %copy-start = (bf16[768,768]{1,0:T(8,128)(2,1)S(1)}, bf16[768,768]{1,0:T(8,128)(2,1)}, u32[]{:S(2)}) copy-start(bf16[768,768]{1,0:T(8,128)(2,1)} %param.19) | copy-start | bytes 3538948
  7.2 68.6 %all-gather.7.cloned.1.call-start = ((), (), s32[]{:S(2)}) async-start(), calls=%async_computation.4 | async-start | bytes 3932160 | tf_op jit(solution)/shard_map/all_gather | solution.py:158
  7.9 244.3 %reduce-scatter.5.cloned.1.call-start = ((), (), s32[]{:S(2)}) async-start(), calls=%async_computation.5 | async-start | bytes 3932160 | tf_op jit(solution)/shard_map/reduce_scatter | solution.py:163
  13.4 67.3 %copy-start.21 = (f32[2048,32]{0,1:T(8,128)}, f32[2048,32]{0,1:T(8,128)S(1)}, u32[]{:S(2)}) copy-start(f32[2048,32]{0,1:T(8,128)S(1)} %get-tuple-element.320) | copy-start | bytes 786436
  187.4 5.5 copy-start.52
  187.4 2.8 copy-start.50
  193.0 59.2 %copy-start.9 = (bf16[512,1,768]{2,0,1:T(8,128)(2,1)S(1)}, bf16[512,1,768]{2,0,1:T(8,128)(2,1)}, u32[]{:S(2)}) copy-start(bf16[512,1,768]{2,0,1:T(8,128)(2,1)} %param.13) | copy-start | bytes 2359300
  193.0 128.3 %all-gather.9.cloned.1.call-start = ((), (), s32[]{:S(2)}) async-start(), calls=%async_computation.6 | async-start | bytes 3932160 | tf_op jit(solution)/shard_map/all_gather | solution.py:174
  252.2 4.2 copy-start.10
  252.2 4.2 copy-start.31
  257.8 138.5 %reduce-scatter.7.cloned.1.call-start = ((), (), s32[]{:S(2)}) async-start(), calls=%async_computation.7 | async-start | bytes 3932160 | tf_op jit(solution)/shard_map/reduce_scatter | solution.py:178
  321.3 5.1 copy-start.44
  321.3 5.1 copy-start.47
  326.4 5.0 copy-start.59
  337.1 130.2 %all-gather.11.cloned.1.call-start = ((), (), s32[]{:S(2)}) async-start(), calls=%async_computation.8 | async-start | bytes 3932160 | tf_op jit(solution)/shard_map/all_gather | solution.py:189
  403.8 139.0 %reduce-scatter.9.cloned.1.call-start = ((), (), s32[]{:S(2)}) async-start(), calls=%async_computation.9 | async-start | bytes 3932160 | tf_op jit(solution)/shard_map/reduce_scatter | solution.py:204
  467.3 9.5 copy-start.46
  476.8 2.7 copy-start.55
  483.5 59.2 %copy-start.11 = (bf16[512,1,768]{2,0,1:T(8,128)(2,1)S(1)}, bf16[512,1,768]{2,0,1:T(8,128)(2,1)}, u32[]{:S(2)}) copy-start(bf16[512,1,768]{2,0,1:T(8,128)(2,1)} %reduce-scatter.5.cloned.1.call-done) | copy-start | bytes 2359300
  483.5 59.2 %copy-start.29 = (f32[512]{0:T(512)S(1)}, f32[512]{0:T(512)}, u32[]{:S(2)}) copy-start(f32[512]{0:T(512)} %copy-done.28) | copy-start | bytes 6148
  483.5 59.2 %copy-start.33 = (f32[512]{0:T(512)S(1)}, f32[512]{0:T(512)}, u32[]{:S(2)}) copy-start(f32[512]{0:T(512)} %copy-done.32) | copy-start | bytes 6148
  483.6 62.6 %copy-start.37 = (f32[512]{0:T(512)S(1)}, f32[512]{0:T(512)}, u32[]{:S(2)}) copy-start(f32[512]{0:T(512)} %copy-done.36) | copy-start | bytes 6148
  483.6 129.4 %all-gather.13.cloned.1.call-start = ((), (), s32[]{:S(2)}) async-start(), calls=%async_computation.10 | async-start | bytes 3932160 | tf_op jit(solution)/shard_map/all_gather | solution.py:214
  542.8 3.4 copy-start.13
  542.8 3.4 copy-start.20
  547.2 65.8 %copy-start.51 = (bf16[192,768]{1,0:T(8,128)(2,1)S(1)}, bf16[192,768]{1,0:T(8,128)(2,1)}, u32[]{:S(2)}) copy-start(bf16[192,768]{1,0:T(8,128)(2,1)} %param.16) | copy-start | bytes 884740
  547.2 69.7 %copy-start.34 = (f32[512]{0:T(512)}, f32[512]{0:T(512)S(1)}, u32[]{:S(2)}) copy-start(f32[512]{0:T(512)S(1)} %negate_multiply_fusion) | copy-start | bytes 6148
  549.5 366.4 %reduce-scatter.11.cloned.1.call-start = ((), (), s32[]{:S(2)}) async-start(), calls=%async_computation.11 | async-start | bytes 3932160 | tf_op jit(solution)/shard_map/reduce_scatter | solution.py:236
  549.5 67.4 %copy-start.53 = (s32[4]{0:T(128)S(1)}, s32[4]{0:T(128)}, u32[]{:S(2)}) copy-start(s32[4]{0:T(128)} %copy-done.52) | copy-start | bytes 52
  627.3 8.7 copy-start.4
  627.3 8.7 copy-start.7
  632.8 3.2 copy-start.3
  654.0 5.1 copy-start.2
  659.1 12.6 %copy-start.5 = (bf16[2048,3,64]{0,2,1:T(8,128)(2,1)S(1)}, bf16[2048,3,64]{0,2,1:T(8,128)(2,1)}, u32[]{:S(2)}) copy-start(bf16[2048,3,64]{0,2,1:T(8,128)(2,1)} %copy-done.4) | copy-start | bytes 2359300 | tf_op jit(solution)/shard_map/while/body/eval_jaxpr/while
  659.1 12.6 %copy-start.8 = (bf16[2048,3,64]{0,2,1:T(8,128)(2,1)S(1)}, bf16[2048,3,64]{0,2,1:T(8,128)(2,1)}, u32[]{:S(2)}) copy-start(bf16[2048,3,64]{0,2,1:T(8,128)(2,1)} %copy-done.7) | copy-start | bytes 2359300 | tf_op jit(solution)/shard_map/while/body/eval_jaxpr/while
  671.7 8.7 copy-start.4
  671.7 8.7 copy-start.7
  677.2 3.2 copy-start.3
  699.0 5.1 copy-start.2
  704.1 13.2 %copy-start.5 = (bf16[2048,3,64]{0,2,1:T(8,128)(2,1)S(1)}, bf16[2048,3,64]{0,2,1:T(8,128)(2,1)}, u32[]{:S(2)}) copy-start(bf16[2048,3,64]{0,2,1:T(8,128)(2,1)} %copy-done.4) | copy-start | bytes 2359300 | tf_op jit(solution)/shard_map/while/body/eval_jaxpr/while
  704.2 13.2 %copy-start.8 = (bf16[2048,3,64]{0,2,1:T(8,128)(2,1)S(1)}, bf16[2048,3,64]{0,2,1:T(8,128)(2,1)}, u32[]{:S(2)}) copy-start(bf16[2048,3,64]{0,2,1:T(8,128)(2,1)} %copy-done.7) | copy-start | bytes 2359300 | tf_op jit(solution)/shard_map/while/body/eval_jaxpr/while
  717.3 8.7 copy-start.4
  717.3 8.7 copy-start.7
  722.8 3.2 copy-start.3
  744.6 5.1 copy-start.2
  749.7 13.2 %copy-start.5 = (bf16[2048,3,64]{0,2,1:T(8,128)(2,1)S(1)}, bf16[2048,3,64]{0,2,1:T(8,128)(2,1)}, u32[]{:S(2)}) copy-start(bf16[2048,3,64]{0,2,1:T(8,128)(2,1)} %copy-done.4) | copy-start | bytes 2359300 | tf_op jit(solution)/shard_map/while/body/eval_jaxpr/while
  749.8 13.2 %copy-start.8 = (bf16[2048,3,64]{0,2,1:T(8,128)(2,1)S(1)}, bf16[2048,3,64]{0,2,1:T(8,128)(2,1)}, u32[]{:S(2)}) copy-start(bf16[2048,3,64]{0,2,1:T(8,128)(2,1)} %copy-done.7) | copy-start | bytes 2359300 | tf_op jit(solution)/shard_map/while/body/eval_jaxpr/while
  762.9 8.6 copy-start.4
  762.9 8.6 copy-start.7
  768.4 3.1 copy-start.3
  790.1 5.1 copy-start.2
  795.2 13.2 %copy-start.5 = (bf16[2048,3,64]{0,2,1:T(8,128)(2,1)S(1)}, bf16[2048,3,64]{0,2,1:T(8,128)(2,1)}, u32[]{:S(2)}) copy-start(bf16[2048,3,64]{0,2,1:T(8,128)(2,1)} %copy-done.4) | copy-start | bytes 2359300 | tf_op jit(solution)/shard_map/while/body/eval_jaxpr/while
  795.2 13.1 %copy-start.8 = (bf16[2048,3,64]{0,2,1:T(8,128)(2,1)S(1)}, bf16[2048,3,64]{0,2,1:T(8,128)(2,1)}, u32[]{:S(2)}) copy-start(bf16[2048,3,64]{0,2,1:T(8,128)(2,1)} %copy-done.7) | copy-start | bytes 2359300 | tf_op jit(solution)/shard_map/while/body/eval_jaxpr/while
  819.7 206.7 %all-reduce.3.cloned.1.call-start = ((), (), s32[]{:S(2)}) async-start(), calls=%async_computation.12 | async-start | bytes 18874368 | tf_op jit(solution)/shard_map/psum | solution.py:244
  819.7 7.1 copy-start.45
  819.7 7.1 copy-start.58
  826.8 4.2 copy-start.56
  831.0 4.2 copy-start.16
  831.0 4.2 copy-start.19
  840.6 75.3 %copy-start.15 = (f32[512,1,768]{2,0,1:T(8,128)S(1)}, f32[512,1,768]{2,0,1:T(8,128)}, u32[]{:S(2)}) copy-start(f32[512,1,768]{2,0,1:T(8,128)} %copy-done.14) | copy-start | bytes 4718596
  840.6 75.3 %copy-start.35 = (f32[512]{0:T(512)S(1)}, f32[512]{0:T(512)}, u32[]{:S(2)}) copy-start(f32[512]{0:T(512)} %copy-done.34) | copy-start | bytes 6148
  1026.4 3.0 copy-start.27
  1026.4 3.8 copy-start.25
  1032.7 3.9 copy-start.1
  (23 other events, 36.4 us)
Sparse Core Ops, SparseCore 0:
  9.6 66.1 all-gather.6
  193.1 59.0 reduce-scatter.4
  257.9 63.3 all-gather.8
  337.2 59.0 reduce-scatter.6
  403.9 63.3 all-gather.10
  483.7 59.0 reduce-scatter.8
  549.6 63.3 all-gather.12
  819.8 63.1 reduce-scatter.10
  887.8 138.5 all-reduce.2
